TPU v7x, 512 devices: a whole 4x4x16 slice. The times are simulated.
512 devices in a mesh: ctx: 8 (over y, z_hi), tp: 64 (over x, z_lo, core).
Axes of the slice: x: 4, y: 4, z: 16 (z_hi: 2, z_lo: 8; z = z_hi * 8 + z_lo), core: 2. Of those that a mesh axis runs over, the one named last changes fastest.
Arguments:
- hidden: bfloat16 [2048, 2048], P(('ctx', 'tp')), may hold values from -6 to 6
- w_in: bfloat16 [2048, 8192], P(None, 'tp'), may hold values from -0.125 to 0.125
- w_bc: bfloat16 [2048, 32], replicated, may hold values from -0.125 to 0.125
- w_dt: bfloat16 [64, 2048], P('tp'), may hold values from -0.125 to 0.125
- dt_bias: float32 [64], P('tp'), may hold values from -5 to -3
- a_log: float32 [64], P('tp'), may hold values from -4.6 to 0
- d_skip: float32 [64], P('tp'), may hold values from 0.5 to 1.5
- conv_w: float32 [4, 4096], P(None, 'tp'), may hold values from -3 to 3
- w_out: bfloat16 [4096, 2048], P('tp'), may hold values from -0.09375 to 0.09375
- d_out: bfloat16 [2048, 2048], P(('ctx', 'tp')), may hold values from -6 to 6
Outputs:
- d_hidden: bfloat16 [2048, 2048], P(('ctx', 'tp'))
- d_w_in: float32 [2048, 8192], P(None, 'tp')
- d_w_out: float32 [4096, 2048], P('tp')
- d_w_bc: float32 [2048, 32], replicated
All inputs are finite; a program needn't handle non-finite values.
Results may differ from a plain program's by a relative error of at most 0.017.
Values may be sent and summed in bfloat16 or wider, within the bound.
A program may use at most 64 MiB of HBM per device.

v0:
```python
import math
import jax
import jax.numpy as jnp
from jax import lax
from jax.sharding import PartitionSpec as P

STATE = 16
CONV = 4
precise = lax.Precision.HIGHEST


def padded(array, sides, width):
    for axis, dim in sides:
        size, length = (lax.axis_size(axis), array.shape[dim])
        up = [(i, (i + 1) % size) for i in range(size - 1)]
        down = [(j, i) for i, j in up]
        last = lax.slice_in_dim(array, length - width, length, axis=dim)
        leading = lax.slice_in_dim(array, 0, width, axis=dim)
        before = lax.ppermute(last, axis, up)
        after = lax.ppermute(leading, axis, down)
        array = jnp.concatenate([before, array, after], axis=dim)
    return array


def entering(array, axis, combine, identity, reverse):
    length, index = (lax.axis_size(axis), lax.axis_index(axis))
    everything = jax.tree.map(lambda part: lax.all_gather(part, axis), array)
    start = jax.tree.map(
        lambda part, zero: jnp.broadcast_to(jnp.asarray(zero, part.dtype), part.shape),
        array,
        identity,
    )

    def step(k, before):
        at = length - 1 - k if reverse else k
        reached = at > index if reverse else at < index
        new = combine(before, jax.tree.map(lambda part: part[at], everything))
        return jax.tree.map(lambda a, b: jnp.where(reached, a, b), new, before)

    return lax.fori_loop(0, length, step, start)


def times_rows(operand_a, operand_b):
    return lax.dot_general(
        operand_a, operand_b, (((1,), (1,)), ((), ())), preferred_element_type=jnp.float32
    )


def across_rows(operand_a, operand_b):
    return lax.dot_general(
        operand_a, operand_b, (((0,), (0,)), ((), ())), preferred_element_type=jnp.float32
    )


def conv_silu(x_ext, conv_w):
    length = x_ext.shape[0] - CONV + 1
    summed = conv_w[0] * x_ext[0:length]
    for shift_k in range(1, CONV):
        summed = summed + conv_w[shift_k] * x_ext[shift_k : shift_k + length]
    return jax.nn.silu(summed)


def block_ssd(conv_out, steps_dt, b_rows, c_rows, decay_rate, state_in):
    positions = conv_out.shape[0]
    log_keep = jnp.cumsum(steps_dt * decay_rate)
    causal = lax.broadcasted_iota(jnp.int32, (positions, positions), 0) >= lax.broadcasted_iota(
        jnp.int32, (positions, positions), 1
    )
    decays = jnp.exp(jnp.where(causal, log_keep[:, None] - log_keep[None, :], -jnp.inf))
    scores = jnp.einsum("in,jn->ij", c_rows, b_rows, precision=precise) * decays
    weighted = steps_dt[:, None] * conv_out
    outputs = jnp.einsum("ij,jp->ip", scores, weighted, precision=precise)
    outputs = outputs + jnp.exp(log_keep)[:, None] * jnp.einsum(
        "in,pn->ip", c_rows, state_in, precision=precise
    )
    remains = jnp.exp(log_keep[-1] - log_keep)
    state_out = jnp.exp(log_keep[-1]) * state_in + jnp.einsum(
        "j,jp,jn->pn", remains, weighted, b_rows, precision=precise
    )
    return (outputs, state_out)


def strand_core(x_ext, gate_in, b_c, dt_raw, state_in, params):
    dt_bias_h, decay_rate, skip_h, conv_w = params
    conv_out = conv_silu(x_ext, conv_w)
    steps_dt = jax.nn.softplus(dt_raw + dt_bias_h)
    outputs, state_out = block_ssd(
        conv_out, steps_dt, b_c[:, :STATE], b_c[:, STATE:], decay_rate, state_in
    )
    gated = (outputs + skip_h * conv_out) * jax.nn.silu(gate_in)
    return (gated, state_out)


def strand_summary(x_ext, b_c, dt_raw, params):
    dt_bias_h, decay_rate, skip_h, conv_w = params
    conv_out = conv_silu(x_ext, conv_w)
    steps_dt = jax.nn.softplus(dt_raw + dt_bias_h)
    log_keep = jnp.cumsum(steps_dt * decay_rate)
    remains = jnp.exp(log_keep[-1] - log_keep) * steps_dt
    local_state = jnp.einsum("j,jp,jn->pn", remains, conv_out, b_c[:, :STATE], precision=precise)
    return (jnp.exp(log_keep[-1]), local_state)


def chain_step(earlier, following):
    return (earlier[0] * following[0], following[0] * earlier[1] + following[1])


def local(hidden, w_in, w_bc, w_dt, dt_bias, a_log, d_skip, conv_w, w_out, d_out):
    own_rows = hidden.shape[0]
    seq_rows = own_rows * lax.axis_size("tp")
    length_all = seq_rows * lax.axis_size("ctx")
    head_dim = w_out.shape[0]
    rim_rows = CONV - 1
    w_pair = jnp.concatenate([w_in, w_in[::-1]], axis=1)
    bc_pair = jnp.concatenate([w_bc, w_bc[::-1]], axis=1)
    dt_pair = jnp.concatenate([w_dt, w_dt[:, ::-1]], axis=0)
    out_pair = jnp.concatenate([w_out, w_out[:, ::-1]], axis=0)
    params = (dt_bias[0], -jnp.exp(a_log[0]), d_skip[0], conv_w)
    gathered = lax.all_gather(hidden, "tp", axis=0, tiled=True)
    projected = jnp.dot(gathered, w_pair, preferred_element_type=jnp.float32).astype(jnp.bfloat16)
    dt_raw = times_rows(gathered, dt_pair)
    b_c_all = jnp.dot(gathered, bc_pair, preferred_element_type=jnp.float32)
    x_both = jnp.concatenate(
        [projected[:, :head_dim], projected[:, 2 * head_dim : 3 * head_dim]], axis=1
    )
    x_halo = padded(x_both, (("ctx", 0),), rim_rows).astype(jnp.float32)
    x_ext = jnp.stack(
        [x_halo[: seq_rows + rim_rows, :head_dim], x_halo[rim_rows:, head_dim:][::-1]]
    )
    gate_in = jnp.stack(
        [projected[:, head_dim : 2 * head_dim], projected[::-1, 3 * head_dim :]]
    ).astype(jnp.float32)
    b_c = jnp.stack([b_c_all[:, : 2 * STATE], b_c_all[::-1, 2 * STATE :]])
    dt_both = jnp.stack([dt_raw[:, 0], dt_raw[::-1, 1]])
    decays, local_states = jax.vmap(strand_summary, in_axes=(0, 0, 0, None))(
        x_ext, b_c, dt_both, params
    )
    identity = (jnp.ones((), jnp.float32), jnp.zeros((head_dim, STATE), jnp.float32))
    fwd_in = entering((decays[0], local_states[0]), "ctx", chain_step, identity, False)[1]
    rev_in = entering((decays[1], local_states[1]), "ctx", chain_step, identity, True)[1]
    states_in = jnp.stack([fwd_in, rev_in])

    def core_both(x_part, gate_part, bc_part, dt_part, state_part):
        return jax.vmap(strand_core, in_axes=(0, 0, 0, 0, 0, None))(
            x_part, gate_part, bc_part, dt_part, state_part, params
        )

    (gated, states_out), pullback = jax.vjp(core_both, x_ext, gate_in, b_c, dt_both, states_in)
    gated_nat = jnp.concatenate([gated[0], gated[1][::-1]], axis=1).astype(jnp.bfloat16)
    portion = lax.all_gather(d_out, "tp", axis=0, tiled=True)
    grads_g = times_rows(portion, out_pair)
    grad_wout = across_rows(gated_nat, portion)
    grad_stack = jnp.stack([grads_g[:, :head_dim], grads_g[::-1, head_dim:]])
    direct = pullback((grad_stack, jnp.zeros_like(states_out)))
    direct_state = direct[4]
    fwd_adj = entering((decays[0], direct_state[0]), "ctx", chain_step, identity, True)[1]
    rev_adj = entering((decays[1], direct_state[1]), "ctx", chain_step, identity, False)[1]
    carried_grads = pullback((jnp.zeros_like(gated), jnp.stack([fwd_adj, rev_adj])))
    grad_x = direct[0] + carried_grads[0]
    grad_gates = direct[1] + carried_grads[1]
    grad_bcs = direct[2] + carried_grads[2]
    grad_dts = direct[3] + carried_grads[3]
    grad_x_rev = grad_x[1][::-1]
    grad_x_local = jnp.concatenate([grad_x[0][rim_rows:], grad_x_rev[:seq_rows]], axis=1)
    outgoing = jnp.concatenate([grad_x[0][:rim_rows], grad_x_rev[seq_rows:]], axis=0)
    incoming = padded(outgoing, (("ctx", 0),), rim_rows)
    grad_x_local = grad_x_local.at[:rim_rows, head_dim:].add(incoming[:rim_rows])
    grad_x_local = grad_x_local.at[seq_rows - rim_rows :, :head_dim].add(incoming[3 * rim_rows :])
    grad_proj = jnp.concatenate(
        [
            grad_x_local[:, :head_dim],
            grad_gates[0],
            grad_x_local[:, head_dim:],
            grad_gates[1][::-1],
        ],
        axis=1,
    ).astype(jnp.bfloat16)
    grad_bc = jnp.concatenate([grad_bcs[0], grad_bcs[1][::-1]], axis=1).astype(jnp.bfloat16)
    grad_dt = jnp.stack([grad_dts[0], grad_dts[1][::-1]], axis=1).astype(jnp.bfloat16)

    def strand_term(which):
        proj_cols = grad_proj[:, which * 2 * head_dim : (which + 1) * 2 * head_dim]
        wide_cols = w_pair[:, which * 2 * head_dim : (which + 1) * 2 * head_dim]
        bc_cols = grad_bc[:, which * 2 * STATE : (which + 1) * 2 * STATE]
        shared_cols = bc_pair[:, which * 2 * STATE : (which + 1) * 2 * STATE]
        dt_cols = grad_dt[:, which : which + 1]
        dt_rows = dt_pair[which : which + 1]
        summed = times_rows(proj_cols, wide_cols) + times_rows(bc_cols, shared_cols)
        return summed + jnp.dot(dt_cols, dt_rows, preferred_element_type=jnp.float32)

    forward_part = lax.psum_scatter(strand_term(0), "tp", scatter_dimension=0, tiled=True)
    reverse_part = lax.psum_scatter(strand_term(1), "tp", scatter_dimension=0, tiled=True)
    d_hidden = (forward_part + reverse_part).astype(jnp.bfloat16)
    scaling = 1.0 / math.sqrt(length_all)
    grad_pair = across_rows(gathered, grad_proj)
    d_w_in = (grad_pair[:, : 2 * head_dim] + grad_pair[::-1, 2 * head_dim :]) * scaling
    d_w_out = (grad_wout[:head_dim] + grad_wout[head_dim:, ::-1]) * scaling
    d_w_in, d_w_out = (
        lax.psum(d_w_in.astype(jnp.bfloat16), "ctx").astype(jnp.float32),
        lax.psum(d_w_out.astype(jnp.bfloat16), "ctx").astype(jnp.float32),
    )
    grad_bpair = across_rows(gathered, grad_bc)
    d_w_bc = lax.psum(
        (grad_bpair[:, : 2 * STATE] + grad_bpair[::-1, 2 * STATE :]) * scaling, ("ctx", "tp")
    )
    return (d_hidden, d_w_in, d_w_out, d_w_bc)


def solution(mesh):
    in_specs = (
        P(("ctx", "tp"), None),
        P(None, "tp"),
        P(),
        P("tp", None),
        P("tp"),
        P("tp"),
        P("tp"),
        P(None, "tp"),
        P("tp", None),
        P(("ctx", "tp"), None),
    )
    out_specs = (P(("ctx", "tp"), None), P(None, "tp"), P("tp", None), P())
    return jax.shard_map(local, mesh=mesh, in_specs=in_specs, out_specs=out_specs, check_vma=False)
```

profile of v0, /device:TPU:4, one launch (start us, length us, event | category | flops | bytes accessed | tf_op | source)
XLA Modules:
  0.0 1343.6 jit_solution(9077498691237861709)
XLA Ops:
  8.7 6.0 rev.53
  14.8 1.3 convert.70
  18.7 1.3 and_reduce_fusion
  20.6 1.4 slice_bitcast_fusion.12
  22.6 6.3 rev.55
  29.0 8.4 rev.49
  37.4 6.3 rev.51
  43.7 1.3 dynamic-slice.21
  45.7 1.3 dynamic-slice.19
  47.0 85.0 %all-gather.7.cloned.1.call-done = bf16[64,4,2048]{2,1,0:T(4,128)(2,1)} async-done(((bf16[1,4,2048]{2,1,0:T(4,128)(2,1)}), bf16[64,4,2048]{2,1,0:T(4,128)(2,1)}) %all-gather.7.cloned.1.call-update) | async-done | bytes 1048592 | tf_op jit(solution)/shard_map/all_gather | solution.py:119
  132.1 1.3 reshape.271
  138.8 2.1 slice_dynamic-update-slice_fusion
  141.6 107.5 %all-gather.5.cloned.1.call-done = bf16[64,4,2048]{2,1,0:T(4,128)(2,1)} async-done(((bf16[1,4,2048]{2,1,0:T(4,128)(2,1)}), bf16[64,4,2048]{2,1,0:T(4,128)(2,1)}) %all-gather.5.cloned.1.call-update) | async-done | bytes 1048592 | tf_op jit(solution)/shard_map/all_gather | solution.py:150
  249.2 1.3 reshape.269
  250.5 1.5 convolution_bitcast_fusion.2
  253.1 8.6 collective-permute-start
  264.7 68.7 %all_gather.29 = f32[8,64,16]{1,2,0:T(8,128)S(1)} all-gather(f32[1,64,16]{1,2,0:T(8,128)S(1)} %get-tuple-element.678), channel_id=1, replica_groups=mesh['ctx'=8,'tp'=64] {'ctx'}, dimensions={0}, use_global_device_ids=true | all-gather | bytes 36864 | tf_op jit(solution)/shard_map/all_gather | solution.py:27
  333.4 41.5 %all-reduce.19 = (f32[8]{0:T(128)S(1)}, f32[8]{0:T(128)S(1)}) all-reduce(f32[8]{0:T(128)} %slice_dynamic-update-slice_fusion, f32[8]{0:T(128)} %copy-done.65), channel_id=1, replica_groups=mesh['ctx'=8,'tp'=64] {'ctx'}, use_global_device_ids=true, to_apply=%add.17 | all-reduce | flops 16 | bytes 128
  374.9 10.2 while.62
  385.1 63.2 %all_gather.31 = f32[8,64,16]{1,2,0:T(8,128)S(1)} all-gather(f32[1,64,16]{1,2,0:T(8,128)S(1)} %get-tuple-element.679), channel_id=1, replica_groups=mesh['ctx'=8,'tp'=64] {'ctx'}, dimensions={0}, use_global_device_ids=true | all-gather | bytes 36864 | tf_op jit(solution)/shard_map/all_gather | solution.py:27
  448.3 10.1 while.63
  461.9 63.1 %all_gather.32 = f32[8,64,16]{1,2,0:T(8,128)S(1)} all-gather(f32[1,64,16]{1,2,0:T(8,128)S(1)} %get-tuple-element.676), channel_id=1, replica_groups=mesh['ctx'=8,'tp'=64] {'ctx'}, dimensions={0}, use_global_device_ids=true | all-gather | bytes 36864 | tf_op jit(solution)/shard_map/all_gather | solution.py:27
  525.1 10.1 while.64
  535.2 63.3 %all_gather.33 = f32[8,64,16]{1,2,0:T(8,128)S(1)} all-gather(f32[1,64,16]{1,2,0:T(8,128)S(1)} %get-tuple-element.677), channel_id=1, replica_groups=mesh['ctx'=8,'tp'=64] {'ctx'}, dimensions={0}, use_global_device_ids=true | all-gather | bytes 36864 | tf_op jit(solution)/shard_map/all_gather | solution.py:27
  598.4 10.2 while.65
  609.9 1.3 fusion.101
  611.2 1.3 fusion.92
  612.6 1.3 fusion.23
  615.1 1.6 fusion.127
  616.6 1.3 fusion.26
  618.7 1.4 multiply_reduce_fusion.3
  622.6 1.3 copy.38
  625.4 1.4 convolution_add_fusion.8
  627.8 2.1 fusion.188
  631.5 2.5 reduce-window.24
  634.9 2.5 reduce-window.26
  643.4 2.5 collective-permute-start.2
  645.9 1.5 collective-permute-start.3
  649.3 1.9 add_select_fusion
  651.2 2.0 scatter-add.6
  653.2 7.6 collective-permute-done.3
  664.2 7.5 rev.61
  674.8 1.7 fusion.31
  678.8 453.5 %all-reduce.28 = bf16[256,2048]{1,0:T(8,128)(2,1)S(1)} all-reduce(f32[256,2048]{1,0:T(8,128)S(1)} %fusion.6), channel_id=3, replica_groups=mesh['ctx'=8,'tp'=64] {'tp'}, use_global_device_ids=true, to_apply=%region_27.28.clone | all-reduce | flops 524288 | bytes 3145728
  1133.0 2.2 copy.41
  1135.2 1.8 convert_element_type.39
  1137.0 198.5 %all-reduce.25.cloned.1.call-done = f32[2048,32]{0,1:T(8,128)} async-done(((f32[2048,32]{0,1:T(8,128)}), f32[2048,32]{0,1:T(8,128)}) %all-reduce.25.cloned.1.call-update) | async-done | bytes 262160 | tf_op jit(solution)/shard_map/psum | solution.py:203
  1335.4 1.7 copy.111
  (321 shorter events, 83.7 us)
Async XLA Ops:
  7.2 126.2 %copy-start.27 = (bf16[1,2048]{1,0:T(2,128)(2,1)S(1)}, bf16[1,2048]{1,0:T(2,128)(2,1)}, u32[]{:S(2)}) copy-start(bf16[1,2048]{1,0:T(2,128)(2,1)} %param.25) | copy-start | bytes 12292
  7.2 124.9 %all-gather.7.cloned.1.call-start = ((), (), s32[]{:S(2)}) async-start(), calls=%async_computation.2 | async-start | bytes 1064960 | tf_op jit(solution)/shard_map/all_gather | solution.py:119
  7.9 241.2 %all-gather.5.cloned.1.call-start = ((), (), s32[]{:S(2)}) async-start(), calls=%async_computation.1 | async-start | bytes 1064960 | tf_op jit(solution)/shard_map/all_gather | solution.py:150
  8.7 1124.3 %all-reduce.27.cloned.1.call-start = ((), (), s32[]{:S(2)}) async-start(), calls=%async_computation.3 | async-start | bytes 1572864 | tf_op jit(solution)/shard_map/psum | solution.py:199
  29.0 106.7 %copy-start.5 = (bf16[2048,32]{0,1:T(8,128)(2,1)}, bf16[2048,32]{0,1:T(8,128)(2,1)S(1)}, u32[]{:S(2)}) copy-start(bf16[2048,32]{0,1:T(8,128)(2,1)S(1)} %rev.55) | copy-start | bytes 393220
  37.4 98.3 %copy-start.4 = (bf16[2048,32]{0,1:T(8,128)(2,1)S(1)}, bf16[2048,32]{0,1:T(8,128)(2,1)}, u32[]{:S(2)}) copy-start(bf16[2048,32]{0,1:T(8,128)(2,1)} %param.24) | copy-start | bytes 393220
  43.7 208.6 %copy-start.2 = (bf16[2048,128]{1,0:T(8,128)(2,1)}, bf16[2048,128]{1,0:T(8,128)(2,1)S(1)}, u32[]{:S(2)}) copy-start(bf16[2048,128]{1,0:T(8,128)(2,1)S(1)} %rev.51) | copy-start | bytes 1572868
  134.6 326.7 %copy-start.33 = (f32[256,1]{0,1:T(1,128)}, f32[256,1]{0,1:T(1,128)S(1)}, u32[]{:S(2)}) copy-start(f32[256,1]{0,1:T(1,128)S(1)} %rev.54) | copy-start | bytes 3076
  135.6 116.4 %copy-start.48 = (f32[1,2,2,128]{3,1,2,0:T(2,128)}, f32[1,2,2,128]{3,1,2,0:T(2,128)S(1)}, u32[]{:S(2)}) copy-start(f32[1,2,2,128]{3,1,2,0:T(2,128)S(1)} %copy.67) | copy-start | bytes 6148
  137.7 114.4 %copy-start.63 = (f32[2]{0:T(128)}, f32[2]{0:T(128)S(1)}, u32[]{:S(2)}) copy-start(f32[2]{0:T(128)S(1)} %slice_reduce_fusion.3) | copy-start | bytes 28
  141.6 110.5 %copy-start.65 = (f32[8]{0:T(128)}, f32[8]{0:T(128)S(1)}, u32[]{:S(2)}) copy-start(f32[8]{0:T(128)S(1)} %slice_dynamic-update-slice_fusion.1) | copy-start | bytes 100
  141.6 110.6 %copy-start = (bf16[2048,128]{1,0:T(8,128)(2,1)S(1)}, bf16[2048,128]{1,0:T(8,128)(2,1)}, u32[]{:S(2)}) copy-start(bf16[2048,128]{1,0:T(8,128)(2,1)} %param.23) | copy-start | bytes 1572868
  252.1 11.7 copy-start.15
  252.3 12.4 copy-start.14
  252.3 206.2 %copy-start.34 = (f32[1,256]{1,0:T(1,128)S(1)}, f32[1,256]{1,0:T(1,128)}, u32[]{:S(2)}) copy-start(f32[1,256]{1,0:T(1,128)} %get-tuple-element.686) | copy-start | bytes 3076
  252.8 206.3 %copy-start.42 = (f32[64]{0:T(128)S(1)}, f32[64]{0:T(128)}, u32[]{:S(2)}) copy-start(f32[64]{0:T(128)} %get-tuple-element.689) | copy-start | bytes 772
  252.8 206.3 %copy-start.44 = (f32[64]{0:T(128)S(1)}, f32[64]{0:T(128)}, u32[]{:S(2)}) copy-start(f32[64]{0:T(128)} %get-tuple-element.690) | copy-start | bytes 772
  252.8 206.3 %copy-start.46 = (f32[64]{0:T(128)S(1)}, f32[64]{0:T(128)}, u32[]{:S(2)}) copy-start(f32[64]{0:T(128)} %get-tuple-element.691) | copy-start | bytes 772
  252.8 206.3 %copy-start.53 = (f32[64]{0:T(128)S(1)}, f32[64]{0:T(128)}, u32[]{:S(2)}) copy-start(f32[64]{0:T(128)} %get-tuple-element.688) | copy-start | bytes 772
  252.8 206.8 %copy-start.21 = (f32[256,32]{0,1:T(8,128)S(1)}, f32[256,32]{0,1:T(8,128)}, u32[]{:S(2)}) copy-start(f32[256,32]{0,1:T(8,128)} %rev.56) | copy-start | bytes 98308
  252.8 206.8 %copy-start.23 = (f32[1,256,32]{1,2,0:T(8,128)S(1)}, f32[1,256,32]{1,2,0:T(8,128)}, u32[]{:S(2)}) copy-start(f32[1,256,32]{1,2,0:T(8,128)} %get-tuple-element.672) | copy-start | bytes 98308
  252.9 205.7 %copy-start.24 = (bf16[1,256,64]{1,2,0:T(8,128)(2,1)}, bf16[1,256,64]{1,2,0:T(8,128)(2,1)S(1)}, u32[]{:S(2)}) copy-start(bf16[1,256,64]{1,2,0:T(8,128)(2,1)S(1)} %get-tuple-element.658) | copy-start | bytes 98308
  253.1 205.5 %copy-start.18 = (bf16[256,64]{0,1:T(8,128)(2,1)}, bf16[256,64]{0,1:T(8,128)(2,1)S(1)}, u32[]{:S(2)}) copy-start(bf16[256,64]{0,1:T(8,128)(2,1)S(1)} %rev.52) | copy-start | bytes 98308
  253.1 205.4 %collective-permute-start = (bf16[3,128]{0,1:T(8,128)(2,1)S(1)}, bf16[3,128]{0,1:T(8,128)(2,1)S(1)}, u32[]{:S(2)}, u32[]{:S(2)}) collective-permute-start(bf16[3,128]{0,1:T(8,128)(2,1)S(1)} %get-tuple-element.670), channel_id=1, source_target_pairs={{0,64},{64,128},{128,192},{192,256},{256,320},{320,384},{384,448},... | collective-permute-start | bytes 2312 | tf_op jit(solution)/shard_map/ppermute | solution.py:19
  261.7 196.8 %collective-permute-start.1 = (bf16[3,128]{0,1:T(8,128)(2,1)S(1)}, bf16[3,128]{0,1:T(8,128)(2,1)S(1)}, u32[]{:S(2)}, u32[]{:S(2)}) collective-permute-start(bf16[3,128]{0,1:T(8,128)(2,1)S(1)} %get-tuple-element.671), channel_id=1, source_target_pairs={{64,0},{128,64},{192,128},{256,192},{320,256},{384,320},{448,384},... | collective-permute-start | bytes 2312 | tf_op jit(solution)/shard_map/ppermute | solution.py:20
  263.7 196.8 %copy-start.64 = (f32[2]{0:T(128)S(1)}, f32[2]{0:T(128)}, u32[]{:S(2)}) copy-start(f32[2]{0:T(128)} %copy-done.63) | copy-start | bytes 28
  263.7 197.5 %copy-start.35 = (f32[1,256]{1,0:T(1,128)S(1)}, f32[1,256]{1,0:T(1,128)}, u32[]{:S(2)}) copy-start(f32[1,256]{1,0:T(1,128)} %get-tuple-element.686) | copy-start | bytes 3076
  458.5 140.0 %copy-start.36 = (f32[2,256]{1,0:T(2,128)}, f32[2,256]{1,0:T(2,128)S(1)}, u32[]{:S(2)}) copy-start(f32[2,256]{1,0:T(2,128)S(1)} %compare_select_fusion.3) | copy-start | bytes 6148
  459.3 151.9 %copy-start.19 = (bf16[256,64]{0,1:T(8,128)(2,1)S(1)}, bf16[256,64]{0,1:T(8,128)(2,1)}, u32[]{:S(2)}) copy-start(bf16[256,64]{0,1:T(8,128)(2,1)} %copy-done.18) | copy-start | bytes 98308
  459.4 151.9 %copy-start.25 = (bf16[1,256,64]{1,2,0:T(8,128)(2,1)S(1)}, bf16[1,256,64]{1,2,0:T(8,128)(2,1)}, u32[]{:S(2)}) copy-start(bf16[1,256,64]{1,2,0:T(8,128)(2,1)} %copy-done.24) | copy-start | bytes 98308
  460.5 152.1 %copy-start.28 = (pred[256,256]{1,0:T(8,128)(4,1)S(1)}, pred[256,256]{1,0:T(8,128)(4,1)}, u32[]{:S(2)}) copy-start(pred[256,256]{1,0:T(8,128)(4,1)} %iota_compare_fusion) | copy-start | bytes 196612
  460.5 152.1 %copy-start.49 = (f32[1,2,2,128]{3,1,2,0:T(2,128)S(1)}, f32[1,2,2,128]{3,1,2,0:T(2,128)}, u32[]{:S(2)}) copy-start(f32[1,2,2,128]{3,1,2,0:T(2,128)} %copy-done.48) | copy-start | bytes 6148
  609.6 9.0 copy-start.22
  625.4 4.7 copy-start.55
  625.4 4.7 copy-start.56
  625.4 4.7 copy-start.57
  625.4 4.7 copy-start.58
  625.4 4.7 copy-start.59
  625.4 4.7 copy-start.60
  625.4 4.7 copy-start.61
  625.4 4.7 copy-start.62
  631.0 31.0 %copy-start.7 = (bf16[256,64]{0,1:T(8,128)(2,1)}, bf16[256,64]{0,1:T(8,128)(2,1)S(1)}, u32[]{:S(2)}) copy-start(bf16[256,64]{0,1:T(8,128)(2,1)S(1)} %rev.58) | copy-start | bytes 98308
  631.3 16.8 %copy-start.16 = (bf16[256,32]{0,1:T(8,128)(2,1)}, bf16[256,32]{0,1:T(8,128)(2,1)S(1)}, u32[]{:S(2)}) copy-start(bf16[256,32]{0,1:T(8,128)(2,1)S(1)} %get-tuple-element.674) | copy-start | bytes 49156
  640.2 7.2 copy-start.51
  640.2 7.2 copy-start.52
  643.4 5.8 collective-permute-start.2
  645.9 14.8 %collective-permute-start.3 = (f32[3,64]{0,1:T(8,128)}, f32[3,64]{0,1:T(8,128)S(1)}, u32[]{:S(2)}, u32[]{:S(2)}) collective-permute-start(f32[3,64]{0,1:T(8,128)} %get-tuple-element.638), channel_id=1, source_target_pairs={{64,0},{128,64},{192,128},{256,192},{320,256},{384,320},{448,384},... | collective-permute-start | bytes 2312 | tf_op jit(solution)/shard_map/ppermute | solution.py:20
  672.7 662.7 %all-reduce.25.cloned.1.call-start = ((), (), s32[]{:S(2)}) async-start(), calls=%async_computation | async-start | bytes 524288 | tf_op jit(solution)/shard_map/psum | solution.py:203
  (29 other events, 83.4 us)
Sparse Core Ops, SparseCore 0:
  10.2 121.8 all-gather.6
  134.2 114.9 all-gather.4
  672.8 200.6 all-reduce.26
  879.7 455.7 all-reduce.24
where the time goes:
time: 1350 us; the launch traced here: 1340 us
  blocking collectives  753 us (56%)
  waiting for transfers between devices  400 us (30%)
  local copies, waits for them, and re-layouts  87.5 us (6%)
  other arithmetic  44.4 us (3%)
  matrix products  25.8 us (2%)
  between operations  17.6 us (1%)
  starting transfers between devices  14 us (1%)
    unnamed x2, blocking collectives  495 us
    all_gather x4, blocking collectives, entering(): everything = jax.tree.map(lambda part: lax.all_gather(part, axis), array)  258 us
    psum x1, waiting for transfers between devices, local(): lax.psum((grad_bpair[:, :2 * STATE] + grad_bpair[::-1, 2 * STATE:]) * sca...  198 us
    all_gather x1, waiting for transfers between devices, local(): portion = lax.all_gather(d_out, 'tp', axis=0, tiled=True)  108 us
    all_gather x1, waiting for transfers between devices, local(): gathered = lax.all_gather(hidden, 'tp', axis=0, tiled=True)  85 us
  transfers between devices with their start and end apart: 8, of which 4 were waited for; matrix products, arithmetic and copies ran while one was open for 6% of the time, Pallas kernels for 0%

commit v1 on v0

--- a/solution.py
+++ b/solution.py
@@ -116,7 +116,9 @@
     dt_pair = jnp.concatenate([w_dt, w_dt[:, ::-1]], axis=0)
     out_pair = jnp.concatenate([w_out, w_out[:, ::-1]], axis=0)
     params = (dt_bias[0], -jnp.exp(a_log[0]), d_skip[0], conv_w)
-    gathered = lax.all_gather(hidden, "tp", axis=0, tiled=True)
+    gathered = jnp.concatenate(
+        lax.all_to_all(jnp.stack([hidden] * lax.axis_size("tp")), "tp", 0, 0), axis=0
+    )
     projected = jnp.dot(gathered, w_pair, preferred_element_type=jnp.float32).astype(jnp.bfloat16)
     dt_raw = times_rows(gathered, dt_pair)
     b_c_all = jnp.dot(gathered, bc_pair, preferred_element_type=jnp.float32)

time: 1350 us -> 1260 us (0.933)
  waiting for transfers between devices: 400 us -> 311 us
  starting transfers between devices: 14 us -> 31.3 us
  local copies, waits for them, and re-layouts: 87.5 us -> 70.4 us
    all_gather x1 -> x0, waiting for transfers between devices: 85 us -> none  [local(): gathered = lax.all_gather(hidden, 'tp', axis=0, tiled=True)]
    all_to_all x0 -> x1, starting transfers between devices: none -> 16.3 us  [local(): lax.all_to_all(jnp.stack([hidden] * lax.axis_size('tp')), 'tp', 0, 0)]
  transfers between devices with their start and end apart: 8 -> 8, of which waited for: 4 -> 3; matrix products, arithmetic and copies ran while one was open for 6% -> 4% of each run, Pallas kernels for 0% -> 0%
where the time goes in v1:
time: 1260 us; the launch traced here: 1250 us
  blocking collectives  755 us (60%)
  waiting for transfers between devices  311 us (25%)
  local copies, waits for them, and re-layouts  70.4 us (6%)
  other arithmetic  43 us (3%)
  starting transfers between devices  31.3 us (2%)
  matrix products  24.8 us (2%)
  between operations  17.6 us (1%)
    unnamed x2, blocking collectives  496 us
    all_gather x4, blocking collectives, entering(): everything = jax.tree.map(lambda part: lax.all_gather(part, axis), array)  259 us
    psum x1, waiting for transfers between devices, local(): lax.psum((grad_bpair[:, :2 * STATE] + grad_bpair[::-1, 2 * STATE:]) * sca...  199 us
    all_gather x1, waiting for transfers between devices, local(): portion = lax.all_gather(d_out, 'tp', axis=0, tiled=True)  104 us
  transfers between devices with their start and end apart: 8, of which 3 were waited for; matrix products, arithmetic and copies ran while one was open for 4% of the time, Pallas kernels for 0%

profile of v1, /device:TPU:4, one launch (start us, length us, event | category | flops | bytes accessed | tf_op | source)
XLA Modules:
  0.0 1253.9 jit_solution(16959894106469017364)
XLA Ops:
  7.2 2.3 stack.55
  9.5 16.3 %all-to-all-start = ((bf16[64,4,2048]{2,1,0:T(4,128)(2,1)}), bf16[64,4,2048]{2,1,0:T(4,128)(2,1)S(1)}, u32[]{:S(2)}, u32[]{:S(2)}) async-start(bf16[64,4,2048]{2,1,0:T(4,128)(2,1)} %stack.55), calls=%async_computation | async-start | bytes 2097152 | tf_op jit(solution)/shard_map/all_to_all | solution.py:120
  26.6 1.5 rev.53
  31.2 1.3 rev.55
  32.6 1.4 rev.49
  34.0 5.1 rev.51
  39.1 1.3 dynamic-slice.21
  41.0 1.3 dynamic-slice.19
  44.8 103.7 %all-gather.3.cloned.1.call-done = bf16[64,4,2048]{2,1,0:T(4,128)(2,1)} async-done(((bf16[1,4,2048]{2,1,0:T(4,128)(2,1)}), bf16[64,4,2048]{2,1,0:T(4,128)(2,1)}) %all-gather.3.cloned.1.call-update) | async-done | bytes 1048592 | tf_op jit(solution)/shard_map/all_gather | solution.py:152
  148.5 1.3 reshape.275
  154.8 1.9 slice_dynamic-update-slice_fusion
  159.6 8.7 collective-permute-start
  168.3 1.3 collective-permute-start.1
  171.2 69.2 %all_gather.25 = f32[8,64,16]{1,2,0:T(8,128)S(1)} all-gather(f32[1,64,16]{1,2,0:T(8,128)S(1)} %get-tuple-element.678), channel_id=1, replica_groups=mesh['ctx'=8,'tp'=64] {'ctx'}, dimensions={0}, use_global_device_ids=true | all-gather | bytes 36864 | tf_op jit(solution)/shard_map/all_gather | solution.py:27
  240.5 40.7 %all-reduce.19 = (f32[8]{0:T(128)S(1)}, f32[8]{0:T(128)S(1)}) all-reduce(f32[8]{0:T(128)} %slice_dynamic-update-slice_fusion, f32[8]{0:T(128)} %copy-done.69), channel_id=1, replica_groups=mesh['ctx'=8,'tp'=64] {'ctx'}, use_global_device_ids=true, to_apply=%add.17 | all-reduce | flops 16 | bytes 128
  281.1 10.0 while.62
  291.1 63.1 %all_gather.27 = f32[8,64,16]{1,2,0:T(8,128)S(1)} all-gather(f32[1,64,16]{1,2,0:T(8,128)S(1)} %get-tuple-element.679), channel_id=1, replica_groups=mesh['ctx'=8,'tp'=64] {'ctx'}, dimensions={0}, use_global_device_ids=true | all-gather | bytes 36864 | tf_op jit(solution)/shard_map/all_gather | solution.py:27
  354.2 10.8 while.63
  368.5 63.1 %all_gather.28 = f32[8,64,16]{1,2,0:T(8,128)S(1)} all-gather(f32[1,64,16]{1,2,0:T(8,128)S(1)} %get-tuple-element.676), channel_id=1, replica_groups=mesh['ctx'=8,'tp'=64] {'ctx'}, dimensions={0}, use_global_device_ids=true | all-gather | bytes 36864 | tf_op jit(solution)/shard_map/all_gather | solution.py:27
  431.5 10.1 while.64
  441.7 63.3 %all_gather.29 = f32[8,64,16]{1,2,0:T(8,128)S(1)} all-gather(f32[1,64,16]{1,2,0:T(8,128)S(1)} %get-tuple-element.677), channel_id=1, replica_groups=mesh['ctx'=8,'tp'=64] {'ctx'}, dimensions={0}, use_global_device_ids=true | all-gather | bytes 36864 | tf_op jit(solution)/shard_map/all_gather | solution.py:27
  504.9 10.2 while.65
  516.3 1.3 fusion.101
  517.7 1.3 fusion.92
  519.0 1.3 fusion.23
  521.5 1.6 fusion.127
  523.1 1.3 fusion.26
  525.1 1.4 multiply_reduce_fusion.3
  527.8 1.3 copy.40
  529.1 1.3 copy.38
  531.9 1.4 convolution_add_fusion.8
  534.3 2.1 fusion.188
  537.9 2.5 reduce-window.24
  541.4 2.5 reduce-window.26
  546.8 1.3 rev.63
  549.9 3.4 collective-permute-start.2
  553.4 1.5 collective-permute-start.3
  556.7 2.0 add_select_fusion
  558.7 2.1 scatter-add.6
  560.8 7.4 collective-permute-done.3
  569.4 1.2 convolution_bitcast_fusion
  571.7 7.5 rev.61
  582.3 1.7 fusion.31
  586.3 455.7 %all-reduce.28 = bf16[256,2048]{1,0:T(8,128)(2,1)S(1)} all-reduce(f32[256,2048]{1,0:T(8,128)S(1)} %fusion.6), channel_id=3, replica_groups=mesh['ctx'=8,'tp'=64] {'tp'}, use_global_device_ids=true, to_apply=%region_27.28.clone | all-reduce | flops 524288 | bytes 3145728
  1042.6 2.2 copy.41
  1044.9 1.8 convert_element_type.39
  1046.6 199.1 %all-reduce.25.cloned.1.call-done = f32[2048,32]{0,1:T(8,128)} async-done(((f32[2048,32]{0,1:T(8,128)}), f32[2048,32]{0,1:T(8,128)}) %all-reduce.25.cloned.1.call-update) | async-done | bytes 262160 | tf_op jit(solution)/shard_map/psum | solution.py:205
  1245.7 1.7 copy.111
  (331 shorter events, 81.0 us)
Async XLA Ops:
  7.2 19.4 %copy-start.30 = (bf16[1,2048]{1,0:T(2,128)(2,1)S(1)}, bf16[1,2048]{1,0:T(2,128)(2,1)}, u32[]{:S(2)}) copy-start(bf16[1,2048]{1,0:T(2,128)(2,1)} %param.25) | copy-start | bytes 12292
  7.2 24.1 %copy-start.5 = (bf16[2048,32]{0,1:T(8,128)(2,1)S(1)}, bf16[2048,32]{0,1:T(8,128)(2,1)}, u32[]{:S(2)}) copy-start(bf16[2048,32]{0,1:T(8,128)(2,1)} %param.24) | copy-start | bytes 393220
  7.2 25.4 %copy-start.16 = (bf16[64,2048]{1,0:T(8,128)(2,1)S(1)}, bf16[64,2048]{1,0:T(8,128)(2,1)}, u32[]{:S(2)}) copy-start(bf16[64,2048]{1,0:T(8,128)(2,1)} %param.30) | copy-start | bytes 786436
  7.2 26.8 %copy-start = (bf16[2048,128]{1,0:T(8,128)(2,1)S(1)}, bf16[2048,128]{1,0:T(8,128)(2,1)}, u32[]{:S(2)}) copy-start(bf16[2048,128]{1,0:T(8,128)(2,1)} %param.23) | copy-start | bytes 1572868
  9.5 33.4 %copy-start.70 = (s32[2]{0:T(128)S(1)}, s32[2]{0:T(128)}, u32[]{:S(2)}) copy-start(s32[2]{0:T(128)} %constant.218.clone.1) | copy-start | bytes 28
  9.5 34.7 %copy-start.58 = (f32[4,64]{1,0:T(4,128)S(1)}, f32[4,64]{1,0:T(4,128)}, u32[]{:S(2)}) copy-start(f32[4,64]{1,0:T(4,128)} %param.29) | copy-start | bytes 3076
  9.5 141.6 %all-to-all-start = ((bf16[64,4,2048]{2,1,0:T(4,128)(2,1)}), bf16[64,4,2048]{2,1,0:T(4,128)(2,1)S(1)}, u32[]{:S(2)}, u32[]{:S(2)}) async-start(bf16[64,4,2048]{2,1,0:T(4,128)(2,1)} %stack.55), calls=%async_computation | async-start | bytes 2097152 | tf_op jit(solution)/shard_map/all_to_all | solution.py:120
  25.8 122.7 %all-gather.3.cloned.1.call-start = ((), (), s32[]{:S(2)}) async-start(), calls=%async_computation.2 | async-start | bytes 1064960 | tf_op jit(solution)/shard_map/all_gather | solution.py:152
  26.5 1016.1 %all-reduce.27.cloned.1.call-start = ((), (), s32[]{:S(2)}) async-start(), calls=%async_computation.3 | async-start | bytes 1572864 | tf_op jit(solution)/shard_map/psum | solution.py:201
  32.6 124.9 %copy-start.6 = (bf16[2048,32]{0,1:T(8,128)(2,1)}, bf16[2048,32]{0,1:T(8,128)(2,1)S(1)}, u32[]{:S(2)}) copy-start(bf16[2048,32]{0,1:T(8,128)(2,1)S(1)} %rev.55) | copy-start | bytes 393220
  151.1 19.2 %copy-start.15 = (f32[256,64]{0,1:T(8,128)}, f32[256,64]{0,1:T(8,128)S(1)}, u32[]{:S(2)}) copy-start(f32[256,64]{0,1:T(8,128)S(1)} %rev.50) | copy-start | bytes 196612
  151.4 7.3 copy-start.1
  151.4 7.3 copy-start.3
  152.5 215.3 %copy-start.36 = (f32[256,1]{0,1:T(1,128)}, f32[256,1]{0,1:T(1,128)S(1)}, u32[]{:S(2)}) copy-start(f32[256,1]{0,1:T(1,128)S(1)} %rev.54) | copy-start | bytes 3076
  153.6 4.9 copy-start.51
  153.8 5.4 copy-start.67
  157.9 12.4 copy-start.17
  158.7 12.5 copy-start.23
  158.7 206.3 %copy-start.37 = (f32[1,256]{1,0:T(1,128)S(1)}, f32[1,256]{1,0:T(1,128)}, u32[]{:S(2)}) copy-start(f32[1,256]{1,0:T(1,128)} %get-tuple-element.686) | copy-start | bytes 3076
  159.2 206.4 %copy-start.45 = (f32[64]{0:T(128)S(1)}, f32[64]{0:T(128)}, u32[]{:S(2)}) copy-start(f32[64]{0:T(128)} %get-tuple-element.689) | copy-start | bytes 772
  159.2 206.4 %copy-start.47 = (f32[64]{0:T(128)S(1)}, f32[64]{0:T(128)}, u32[]{:S(2)}) copy-start(f32[64]{0:T(128)} %get-tuple-element.690) | copy-start | bytes 772
  159.3 206.4 %copy-start.49 = (f32[64]{0:T(128)S(1)}, f32[64]{0:T(128)}, u32[]{:S(2)}) copy-start(f32[64]{0:T(128)} %get-tuple-element.691) | copy-start | bytes 772
  159.3 206.4 %copy-start.56 = (f32[64]{0:T(128)S(1)}, f32[64]{0:T(128)}, u32[]{:S(2)}) copy-start(f32[64]{0:T(128)} %get-tuple-element.688) | copy-start | bytes 772
  159.3 206.9 %copy-start.26 = (f32[1,256,32]{1,2,0:T(8,128)S(1)}, f32[1,256,32]{1,2,0:T(8,128)}, u32[]{:S(2)}) copy-start(f32[1,256,32]{1,2,0:T(8,128)} %get-tuple-element.672) | copy-start | bytes 98308
  159.3 205.8 %copy-start.27 = (bf16[1,256,64]{1,2,0:T(8,128)(2,1)}, bf16[1,256,64]{1,2,0:T(8,128)(2,1)S(1)}, u32[]{:S(2)}) copy-start(bf16[1,256,64]{1,2,0:T(8,128)(2,1)S(1)} %get-tuple-element.658) | copy-start | bytes 98308
  159.5 205.8 %copy-start.20 = (bf16[256,64]{0,1:T(8,128)(2,1)}, bf16[256,64]{0,1:T(8,128)(2,1)S(1)}, u32[]{:S(2)}) copy-start(bf16[256,64]{0,1:T(8,128)(2,1)S(1)} %rev.52) | copy-start | bytes 98308
  159.6 205.5 %collective-permute-start = (bf16[3,128]{0,1:T(8,128)(2,1)S(1)}, bf16[3,128]{0,1:T(8,128)(2,1)S(1)}, u32[]{:S(2)}, u32[]{:S(2)}) collective-permute-start(bf16[3,128]{0,1:T(8,128)(2,1)S(1)} %get-tuple-element.670), channel_id=1, source_target_pairs={{0,64},{64,128},{128,192},{192,256},{256,320},{320,384},{384,448},... | collective-permute-start | bytes 2312 | tf_op jit(solution)/shard_map/ppermute | solution.py:19
  168.3 196.8 %collective-permute-start.1 = (bf16[3,128]{0,1:T(8,128)(2,1)S(1)}, bf16[3,128]{0,1:T(8,128)(2,1)S(1)}, u32[]{:S(2)}, u32[]{:S(2)}) collective-permute-start(bf16[3,128]{0,1:T(8,128)(2,1)S(1)} %get-tuple-element.671), channel_id=1, source_target_pairs={{64,0},{128,64},{192,128},{256,192},{320,256},{384,320},{448,384},... | collective-permute-start | bytes 2312 | tf_op jit(solution)/shard_map/ppermute | solution.py:20
  170.3 196.7 %copy-start.68 = (f32[2]{0:T(128)S(1)}, f32[2]{0:T(128)}, u32[]{:S(2)}) copy-start(f32[2]{0:T(128)} %copy-done.67) | copy-start | bytes 28
  170.3 197.5 %copy-start.38 = (f32[1,256]{1,0:T(1,128)S(1)}, f32[1,256]{1,0:T(1,128)}, u32[]{:S(2)}) copy-start(f32[1,256]{1,0:T(1,128)} %get-tuple-element.686) | copy-start | bytes 3076
  171.2 194.9 %copy-start.24 = (f32[256,32]{0,1:T(8,128)S(1)}, f32[256,32]{0,1:T(8,128)}, u32[]{:S(2)}) copy-start(f32[256,32]{0,1:T(8,128)} %copy-done.23) | copy-start | bytes 98308
  365.0 139.9 %copy-start.39 = (f32[2,256]{1,0:T(2,128)}, f32[2,256]{1,0:T(2,128)S(1)}, u32[]{:S(2)}) copy-start(f32[2,256]{1,0:T(2,128)S(1)} %compare_select_fusion.3) | copy-start | bytes 6148
  365.9 151.8 %copy-start.21 = (bf16[256,64]{0,1:T(8,128)(2,1)S(1)}, bf16[256,64]{0,1:T(8,128)(2,1)}, u32[]{:S(2)}) copy-start(bf16[256,64]{0,1:T(8,128)(2,1)} %copy-done.20) | copy-start | bytes 98308
  365.9 151.8 %copy-start.28 = (bf16[1,256,64]{1,2,0:T(8,128)(2,1)S(1)}, bf16[1,256,64]{1,2,0:T(8,128)(2,1)}, u32[]{:S(2)}) copy-start(bf16[1,256,64]{1,2,0:T(8,128)(2,1)} %copy-done.27) | copy-start | bytes 98308
  367.0 152.0 %copy-start.31 = (pred[256,256]{1,0:T(8,128)(4,1)S(1)}, pred[256,256]{1,0:T(8,128)(4,1)}, u32[]{:S(2)}) copy-start(pred[256,256]{1,0:T(8,128)(4,1)} %iota_compare_fusion) | copy-start | bytes 196612
  367.0 152.0 %copy-start.52 = (f32[1,2,2,128]{3,1,2,0:T(2,128)S(1)}, f32[1,2,2,128]{3,1,2,0:T(2,128)}, u32[]{:S(2)}) copy-start(f32[1,2,2,128]{3,1,2,0:T(2,128)} %copy-done.51) | copy-start | bytes 6148
  516.1 9.0 copy-start.25
  531.8 4.7 copy-start.61
  531.8 4.7 copy-start.62
  531.8 4.7 copy-start.63
  531.8 4.7 copy-start.64
  537.4 32.0 %copy-start.8 = (bf16[256,64]{0,1:T(8,128)(2,1)}, bf16[256,64]{0,1:T(8,128)(2,1)S(1)}, u32[]{:S(2)}) copy-start(bf16[256,64]{0,1:T(8,128)(2,1)S(1)} %rev.58) | copy-start | bytes 98308
  537.7 17.8 %copy-start.18 = (bf16[256,32]{0,1:T(8,128)(2,1)}, bf16[256,32]{0,1:T(8,128)(2,1)S(1)}, u32[]{:S(2)}) copy-start(bf16[256,32]{0,1:T(8,128)(2,1)S(1)} %get-tuple-element.674) | copy-start | bytes 49156
  546.7 8.2 copy-start.54
  546.7 8.2 copy-start.55
  549.9 6.8 collective-permute-start.2
  553.4 14.8 %collective-permute-start.3 = (f32[3,64]{0,1:T(8,128)}, f32[3,64]{0,1:T(8,128)S(1)}, u32[]{:S(2)}, u32[]{:S(2)}) collective-permute-start(f32[3,64]{0,1:T(8,128)} %get-tuple-element.638), channel_id=1, source_target_pairs={{64,0},{128,64},{192,128},{256,192},{320,256},{384,320},{448,384},... | collective-permute-start | bytes 2312 | tf_op jit(solution)/shard_map/ppermute | solution.py:20
  580.1 665.5 %all-reduce.25.cloned.1.call-start = ((), (), s32[]{:S(2)}) async-start(), calls=%async_computation.1 | async-start | bytes 524288 | tf_op jit(solution)/shard_map/psum | solution.py:205
  (34 other events, 103.8 us)
Sparse Core Ops, SparseCore 0:
  28.8 119.6 all-gather.2
  580.3 201.7 all-reduce.26
  788.4 457.2 all-reduce.24
